TPU v7x, 256 devices: a whole 4x4x8 slice. The times are simulated.
256 devices in a mesh: dp: 8 (over y, core), ctx: 32 (over x, z).
Axes of the slice: x: 4, y: 4, z: 8, core: 2. Of those that a mesh axis runs over, the one named last changes fastest.
Arguments:
- query_rows: bfloat16 [8, 16384, 1024], P('dp', 'ctx'), may hold values from -6 to 6
- key_rows: bfloat16 [8, 16384, 1024], P('dp', 'ctx'), may hold values from -6 to 6
- value_rows: bfloat16 [8, 16384, 1024], P('dp', 'ctx'), may hold values from -6 to 6
- query_gain: float32 [128], replicated, may hold values from 0.5 to 1.5
- key_gain: float32 [128], replicated, may hold values from 0.5 to 1.5
- selected: int32 [8, 32, 3], P('dp', 'ctx'), may hold values from 0 to 30, as said below
- output_grad: bfloat16 [8, 16384, 1024], P('dp', 'ctx'), may hold values from -6 to 6
Outputs:
- attended: bfloat16 [8, 16384, 1024], P('dp', 'ctx')
- query_grad: bfloat16 [8, 16384, 1024], P('dp', 'ctx')
- key_grad: bfloat16 [8, 16384, 1024], P('dp', 'ctx')
- value_grad: bfloat16 [8, 16384, 1024], P('dp', 'ctx')
- query_gain_grad: float32 [128], replicated
- key_gain_grad: float32 [128], replicated
Inputs may be any that keep to these rules, and one draw needn't show every extreme that they name: selected[b, i, 0] is 0 for every query block i, and selected[b, i, 2] is i - 1 for every i >= 2. Every entry of row i lies in 0 to i, and an entry equal to i names no block. Entries below i are distinct within a row. For i >= 3 every entry is below i.
All inputs are finite; a program needn't handle non-finite values.
Results may differ from a plain program's by a relative error of at most 0.012.
Values may be sent and summed in bfloat16 or wider, within the bound.
A program may use at most 128 MiB of HBM per device.

v0:
```python
import jax
import jax.numpy as jnp
from jax import lax
from jax.sharding import PartitionSpec as P


def head_norm(inputs, gain_vector):
    head_dim = gain_vector.shape[0]
    shaped = inputs.reshape(inputs.shape[:-1] + (inputs.shape[-1] // head_dim, head_dim))
    factor = lax.rsqrt(jnp.mean(shaped * shaped, axis=-1, keepdims=True) + 1e-06)
    return (shaped * factor * gain_vector).reshape(inputs.shape)


def attend(query_block, key_list, value_list, visible_list, grad_block, score_scale):
    weight_list = []
    row_total = 0.0
    for key_block, visible in zip(key_list, visible_list):
        scores = jnp.einsum(
            "qhd,khd->hqk", query_block, key_block, preferred_element_type=jnp.float32
        )
        weights = jnp.exp(score_scale * scores) * visible
        row_total = row_total + jnp.sum(weights, axis=-1)
        weight_list.append(weights)
    prob_list = [(weights / row_total[:, :, None]).astype(jnp.bfloat16) for weights in weight_list]
    accumulated = 0.0
    for prob_block, value_block in zip(prob_list, value_list):
        accumulated = accumulated + jnp.einsum(
            "hqk,khd->qhd", prob_block, value_block, preferred_element_type=jnp.float32
        )
    output = accumulated.astype(jnp.bfloat16)
    row_delta = jnp.einsum("qhd,qhd->hq", grad_block, output, preferred_element_type=jnp.float32)
    query_grad = 0.0
    key_terms = []
    value_terms = []
    for prob_block, key_block, value_block in zip(prob_list, key_list, value_list):
        grad_probs = jnp.einsum(
            "qhd,khd->hqk", grad_block, value_block, preferred_element_type=jnp.float32
        )
        grad_scores = (
            prob_block.astype(jnp.float32) * (grad_probs - row_delta[:, :, None])
        ).astype(jnp.bfloat16)
        value_terms.append(
            jnp.einsum("hqk,qhd->khd", prob_block, grad_block, preferred_element_type=jnp.float32)
        )
        key_terms.append(
            score_scale
            * jnp.einsum(
                "hqk,qhd->khd", grad_scores, query_block, preferred_element_type=jnp.float32
            )
        )
        query_grad = query_grad + score_scale * jnp.einsum(
            "hqk,khd->qhd", grad_scores, key_block, preferred_element_type=jnp.float32
        )
    return (output, query_grad, key_terms, value_terms)


def local(query_rows, key_rows, value_rows, query_gain, key_gain, selected, output_grad):
    ctx_count = lax.axis_size("ctx")
    device_index = lax.axis_index("ctx")
    local_count = selected.shape[1]
    slot_total = selected.shape[2]
    token_count = query_rows.shape[1]
    model_width = query_rows.shape[2]
    head_dim = query_gain.shape[0]
    head_count = model_width // head_dim
    block_size = token_count // local_count
    slice_rows = block_size // ctx_count
    block_count = local_count * ctx_count
    score_scale = head_dim ** (-0.5)

    def heads_view(block_array):
        return block_array.reshape(block_size, head_count, head_dim)

    choice_table = lax.all_gather(selected[0], "ctx", axis=0, tiled=True)
    query_float = query_rows[0].astype(jnp.float32)
    key_float = key_rows[0].astype(jnp.float32)
    query_normed = head_norm(query_float, query_gain).astype(jnp.bfloat16)
    key_normed = head_norm(key_float, key_gain).astype(jnp.bfloat16)
    value_local = value_rows[0]
    holder_keys, holder_values = (
        lax.all_to_all(
            key_normed.reshape(local_count, block_size, model_width),
            "ctx",
            split_axis=1,
            concat_axis=0,
            tiled=True,
        ),
        lax.all_to_all(
            value_local.reshape(local_count, block_size, model_width),
            "ctx",
            split_axis=1,
            concat_axis=0,
            tiled=True,
        ),
    )
    first_slot = 0
    fetched_keys, fetched_values = (
        lax.all_to_all(holder_keys[choice_table], "ctx", split_axis=0, concat_axis=2, tiled=True),
        lax.all_to_all(holder_values[choice_table], "ctx", split_axis=0, concat_axis=2, tiled=True),
    )
    positions = jnp.arange(block_size)
    causal = (positions[None, :] <= positions[:, None]).astype(jnp.float32)[None]
    own_block = device_index * local_count + 0
    chosen = selected[0, 0]
    key_list = [heads_view(key_normed)]
    value_list = [heads_view(value_local)]
    visible_list = [causal]
    for slot_index in range(slot_total):
        fetched_slot = slot_index - first_slot
        key_list.append(heads_view(fetched_keys[0, fetched_slot]))
        value_list.append(heads_view(fetched_values[0, fetched_slot]))
        visible_list.append((chosen[slot_index] != own_block).astype(jnp.float32))
    output, query_grad, key_terms, value_terms = attend(
        heads_view(query_normed),
        key_list,
        value_list,
        visible_list,
        heads_view(output_grad[0, 0:block_size]),
        score_scale,
    )
    outputs = output.reshape(block_size, model_width)
    query_grads = query_grad.reshape(block_size, model_width)
    own_keys = [key_terms[0].reshape(block_size, model_width)]
    own_values = [value_terms[0].reshape(block_size, model_width)]
    remote_keys = [
        jnp.stack([grad_term.astype(jnp.bfloat16) for grad_term in key_terms[1:]]).reshape(
            slot_total, block_size, model_width
        )
    ]
    remote_values = [
        jnp.stack([grad_term.astype(jnp.bfloat16) for grad_term in value_terms[1:]]).reshape(
            slot_total, block_size, model_width
        )
    ]
    remote_key_all = jnp.stack(remote_keys)
    remote_value_all = jnp.stack(remote_values)
    back_keys, back_values = (
        lax.all_to_all(remote_key_all, "ctx", split_axis=2, concat_axis=0, tiled=True),
        lax.all_to_all(remote_value_all, "ctx", split_axis=2, concat_axis=0, tiled=True),
    )
    selector = (choice_table.reshape(-1)[None, :] == jnp.arange(block_count)[:, None]).astype(
        jnp.bfloat16
    )
    summed_keys = jnp.dot(
        selector,
        back_keys.reshape(block_count * slot_total, slice_rows * model_width),
        preferred_element_type=jnp.float32,
    )
    summed_values = jnp.dot(
        selector,
        back_values.reshape(block_count * slot_total, slice_rows * model_width),
        preferred_element_type=jnp.float32,
    )
    summed_keys = summed_keys.reshape(block_count, slice_rows, model_width)
    summed_values = summed_values.reshape(block_count, slice_rows, model_width)
    collected_keys, collected_values = (
        lax.all_to_all(
            summed_keys.astype(jnp.bfloat16), "ctx", split_axis=0, concat_axis=1, tiled=True
        ),
        lax.all_to_all(
            summed_values.astype(jnp.bfloat16), "ctx", split_axis=0, concat_axis=1, tiled=True
        ),
    )
    remote_key_total = collected_keys.astype(jnp.float32)
    remote_value_total = collected_values.astype(jnp.float32)
    key_total = (jnp.stack(own_keys) + remote_key_total).reshape(token_count, model_width)
    value_grad = (
        (jnp.stack(own_values) + remote_value_total)
        .reshape(token_count, model_width)
        .astype(jnp.bfloat16)
    )
    _, query_pull = jax.vjp(head_norm, query_float, query_gain)
    query_grad, query_gain_part = query_pull(query_grads)
    _, key_pull = jax.vjp(head_norm, key_float, key_gain)
    key_grad, key_gain_part = key_pull(key_total)
    query_gain_grad, key_gain_grad = lax.psum((query_gain_part, key_gain_part), ("dp", "ctx"))
    return (
        outputs[None],
        query_grad.astype(jnp.bfloat16)[None],
        key_grad.astype(jnp.bfloat16)[None],
        value_grad[None],
        query_gain_grad,
        key_gain_grad,
    )


def solution(mesh):
    in_specs = (
        P("dp", "ctx", None),
        P("dp", "ctx", None),
        P("dp", "ctx", None),
        P(),
        P(),
        P("dp", "ctx", None),
        P("dp", "ctx", None),
    )
    out_specs = (
        P("dp", "ctx", None),
        P("dp", "ctx", None),
        P("dp", "ctx", None),
        P("dp", "ctx", None),
        P(),
        P(),
    )
    return jax.shard_map(local, mesh=mesh, in_specs=in_specs, out_specs=out_specs, check_vma=False)
```

profile of v0, /device:TPU:1, one launch (start us, length us, event | category | flops | bytes accessed | tf_op | source)
XLA Modules:
  0.0 716.8 jit_solution(10691990284044521353)
XLA Ops:
  13.3 9.1 %reduce.7 = bf16[512,1024]{1,0:T(8,128)(2,1)} reduce(bf16[512,1,1024]{2,1,0:T(2,128)(2,1)} %bitcast.237, bf16[]{:T(256)} %broadcast.153), dimensions={1}, to_apply=%bitcast.200.reduce_sub_computation | reduce | bytes 2097154
  25.0 12.2 %all-to-all-start = ((bf16[32,2,8192]{2,1,0:T(2,128)(2,1)}), bf16[32,2,8192]{2,1,0:T(2,128)(2,1)}, u32[]{:S(2)}, u32[]{:S(2)}) async-start(bf16[32,2,8192]{2,1,0:T(2,128)(2,1)} %reshape.270), calls=%async_computation | async-start | bytes 2097152 | tf_op jit(solution)/shard_map/all_to_all | solution.py:81
  40.1 8.0 %reduce.6 = bf16[512,1024]{1,0:T(8,128)(2,1)S(1)} reduce(bf16[512,1,1024]{2,1,0:T(2,128)(2,1)} %bitcast.238, bf16[]{:T(256)} %broadcast.153), dimensions={1}, to_apply=%bitcast.199.reduce_sub_computation | reduce | bytes 2097154
  49.7 12.0 %all-to-all-done = bf16[32,2,8192]{2,1,0:T(2,128)(2,1)} async-done(((bf16[32,2,8192]{2,1,0:T(2,128)(2,1)}), bf16[32,2,8192]{2,1,0:T(2,128)(2,1)}, u32[]{:S(2)}, u32[]{:S(2)}) %all-to-all-start) | async-done | bytes 1048608 | tf_op jit(solution)/shard_map/all_to_all | solution.py:81
  61.7 8.7 %all-to-all-start.2 = ((bf16[32,2,8192]{2,1,0:T(2,128)(2,1)}), bf16[32,2,8192]{2,1,0:T(2,128)(2,1)}, u32[]{:S(2)}, u32[]{:S(2)}) async-start(bf16[32,2,8192]{2,1,0:T(2,128)(2,1)} %reshape.268), calls=%async_computation.2 | async-start | bytes 2097152 | tf_op jit(solution)/shard_map/all_to_all | solution.py:88
  70.5 48.7 %all-gather = s32[32,1,3]{2,1,0:T(1,128)S(1)} all-gather(s32[1,1,3]{2,1,0:T(1,128)S(1)} %copy-done.32), channel_id=2, replica_groups=mesh['dp'=8,'ctx'=32] {'ctx'}, dimensions={0}, use_global_device_ids=true | all-gather | bytes 396 | tf_op jit(solution)/shard_map/all_gather | solution.py:74
  119.5 5.8 reshape.271
  129.8 5.3 all-to-all-start.1
  135.1 5.8 reshape.269
  145.5 54.6 %all-to-all-done.1 = bf16[32,3,16,1024]{3,2,1,0:T(8,128)(2,1)} async-done(((bf16[32,3,16,1024]{3,2,1,0:T(8,128)(2,1)}), bf16[32,3,16,1024]{3,2,1,0:T(8,128)(2,1)}, u32[]{:S(2)}, u32[]{:S(2)}) %all-to-all-start.1) | async-done | bytes 3145760 | tf_op jit(solution)/shard_map/all_to_all | solution.py:98
  200.1 5.4 all-to-all-start.3
  232.8 34.6 %all-to-all-done.3 = bf16[32,3,16,1024]{3,2,1,0:T(8,128)(2,1)} async-done(((bf16[32,3,16,1024]{3,2,1,0:T(8,128)(2,1)}), bf16[32,3,16,1024]{3,2,1,0:T(8,128)(2,1)}, u32[]{:S(2)}, u32[]{:S(2)}) %all-to-all-start.3) | async-done | bytes 3145760 | tf_op jit(solution)/shard_map/all_to_all | solution.py:99
  278.4 6.3 fusion.6
  284.8 5.1 fusion.5
  289.9 5.0 fusion.4
  295.0 11.9 %divide_convert_fusion.3 = (bf16[8,512,512]{1,2,0:T(8,128)(2,1)S(1)}, bf16[8,512,512]{1,2,0:T(8,128)(2,1)S(1)}, bf16[8,512,512]{1,2,0:T(8,128)(2,1)S(1)}, bf16[8,512,512]{1,2,0:T(8,128)(2,1)S(1)}) fusion(f32[8,512,512]{1,2,0:T(8,128)S(1)} %bitcast.207, f32[8,512]{1,0:T(8,128)S(1)} %add_add_fusion.2, f32[512,512]{0,1:T(8,128)} %copy-done.14, ...), kind=kLoop, calls=%fused_computation.12 | loop fusion | flops 33554432 | bytes 51396620 | tf_op jit(solution)/shard_map/convert_element_type | solution.py:24
  336.6 6.0 copy.538
  347.3 6.0 copy.539
  358.0 6.2 copy.540
  364.1 9.6 %pad_maximum_fusion = bf16[1,3,512,1024]{3,1,0,2:T(4,128)(2,1)} fusion(bf16[1,1,512,1024]{3,1,0,2:T(2,128)(2,1)} %copy.540, bf16[1,1,512,1024]{3,1,0,2:T(2,128)(2,1)} %copy.539, bf16[1,1,512,1024]{3,1,0,2:T(2,128)(2,1)} %copy.538), kind=kLoop, calls=%fused_computation.21 | loop fusion | flops 9437184 | bytes 6291456 | tf_op jit(solution)/shard_map/stack | solution.py:126
  373.8 7.3 %all-to-all-start.4 = ((bf16[1,3,512,1024]{3,1,0,2:T(4,128)(2,1)}), bf16[1,3,512,1024]{3,1,0,2:T(4,128)(2,1)}, u32[]{:S(2)}, u32[]{:S(2)}) async-start(bf16[1,3,512,1024]{3,1,0,2:T(4,128)(2,1)} %pad_maximum_fusion), calls=%async_computation.4 | async-start | bytes 8388608 | tf_op jit(solution)/shard_map/all_to_all | solution.py:138
  385.7 6.1 copy.556
  396.4 6.0 copy.557
  407.1 6.1 copy.558
  413.2 9.7 %pad_maximum_fusion.1 = bf16[1,3,512,1024]{3,1,0,2:T(4,128)(2,1)} fusion(bf16[1,1,512,1024]{3,1,0,2:T(2,128)(2,1)} %copy.558, bf16[1,1,512,1024]{3,1,0,2:T(2,128)(2,1)} %copy.557, bf16[1,1,512,1024]{3,1,0,2:T(2,128)(2,1)} %copy.556), kind=kLoop, calls=%fused_computation.22 | loop fusion | flops 9437184 | bytes 6291456 | tf_op jit(solution)/shard_map/stack | solution.py:131
  422.9 42.1 %all-to-all-done.4 = bf16[1,3,512,1024]{3,1,0,2:T(4,128)(2,1)} async-done(((bf16[1,3,512,1024]{3,1,0,2:T(4,128)(2,1)}), bf16[1,3,512,1024]{3,1,0,2:T(4,128)(2,1)}, u32[]{:S(2)}, u32[]{:S(2)}) %all-to-all-start.4) | async-done | bytes 3145760 | tf_op jit(solution)/shard_map/all_to_all | solution.py:138
  465.0 9.8 %all-to-all-start.6 = ((bf16[1,3,512,1024]{3,1,0,2:T(4,128)(2,1)}), bf16[1,3,512,1024]{3,1,0,2:T(4,128)(2,1)}, u32[]{:S(2)}, u32[]{:S(2)}) async-start(bf16[1,3,512,1024]{3,1,0,2:T(4,128)(2,1)} %pad_maximum_fusion.1), calls=%async_computation.6 | async-start | bytes 8388608 | tf_op jit(solution)/shard_map/all_to_all | solution.py:139
  489.7 71.2 %all-to-all-done.6 = bf16[1,3,512,1024]{3,1,0,2:T(4,128)(2,1)} async-done(((bf16[1,3,512,1024]{3,1,0,2:T(4,128)(2,1)}), bf16[1,3,512,1024]{3,1,0,2:T(4,128)(2,1)}, u32[]{:S(2)}, u32[]{:S(2)}) %all-to-all-start.6) | async-done | bytes 3145760 | tf_op jit(solution)/shard_map/all_to_all | solution.py:139
  560.9 7.3 %all-to-all-start.5 = ((bf16[32,16,1024]{2,1,0:T(8,128)(2,1)}), bf16[32,16,1024]{2,1,0:T(8,128)(2,1)}, u32[]{:S(2)}, u32[]{:S(2)}) async-start(bf16[32,16,1024]{2,1,0:T(8,128)(2,1)} %copy.544), calls=%async_computation.5 | async-start | bytes 2097152 | tf_op jit(solution)/shard_map/all_to_all | solution.py:157
  590.0 9.6 %all-to-all-start.7 = ((bf16[32,16,1024]{2,1,0:T(8,128)(2,1)}), bf16[32,16,1024]{2,1,0:T(8,128)(2,1)S(1)}, u32[]{:S(2)}, u32[]{:S(2)}) async-start(bf16[32,16,1024]{2,1,0:T(8,128)(2,1)} %copy.562), calls=%async_computation.7 | async-start | bytes 2097152 | tf_op jit(solution)/shard_map/all_to_all | solution.py:160
  620.9 5.2 multiply_reduce_fusion.1
  630.0 85.0 %all-reduce = (f32[128]{0:T(128)}, f32[128]{0:T(128)}) all-reduce(f32[128]{0:T(128)S(1)} %get-tuple-element.56, f32[128]{0:T(128)S(1)} %get-tuple-element.54), channel_id=1, replica_groups=mesh['dp'=8,'ctx'=32] {'dp','ctx'}, use_global_device_ids=true, to_apply=%region_9.0 | all-reduce | flops 256 | bytes 2048 | tf_op jit(solution)/shard_map/psum | solution.py:176
  (165 shorter events, 181.3 us)
Async XLA Ops:
  3.3 4.5 copy-start.31
  3.3 4.5 copy-start.26
  13.3 23.9 %copy-start.27 = (bf16[1,512,1024]{2,1,0:T(8,128)(2,1)S(1)}, bf16[1,512,1024]{2,1,0:T(8,128)(2,1)}, u32[]{:S(2)}) copy-start(bf16[1,512,1024]{2,1,0:T(8,128)(2,1)} %param.9) | copy-start | bytes 3145732
  25.0 36.8 %all-to-all-start = ((bf16[32,2,8192]{2,1,0:T(2,128)(2,1)}), bf16[32,2,8192]{2,1,0:T(2,128)(2,1)}, u32[]{:S(2)}, u32[]{:S(2)}) async-start(bf16[32,2,8192]{2,1,0:T(2,128)(2,1)} %reshape.270), calls=%async_computation | async-start | bytes 2097152 | tf_op jit(solution)/shard_map/all_to_all | solution.py:81
  40.1 30.4 %copy-start.32 = (s32[1,1,3]{2,1,0:T(1,128)S(1)}, s32[1,1,3]{2,1,0:T(1,128)}, u32[]{:S(2)}) copy-start(s32[1,1,3]{2,1,0:T(1,128)} %param.12) | copy-start | bytes 40
  61.7 68.1 %all-to-all-start.2 = ((bf16[32,2,8192]{2,1,0:T(2,128)(2,1)}), bf16[32,2,8192]{2,1,0:T(2,128)(2,1)}, u32[]{:S(2)}, u32[]{:S(2)}) async-start(bf16[32,2,8192]{2,1,0:T(2,128)(2,1)} %reshape.268), calls=%async_computation.2 | async-start | bytes 2097152 | tf_op jit(solution)/shard_map/all_to_all | solution.py:88
  129.8 70.3 %all-to-all-start.1 = ((bf16[32,3,16,1024]{3,2,1,0:T(8,128)(2,1)}), bf16[32,3,16,1024]{3,2,1,0:T(8,128)(2,1)}, u32[]{:S(2)}, u32[]{:S(2)}) async-start(bf16[32,3,16,1024]{3,2,1,0:T(8,128)(2,1)} %bitcast.215), calls=%async_computation.1 | async-start | bytes 6291456 | tf_op jit(solution)/shard_map/all_to_all | solution.py:98
  200.1 67.3 %all-to-all-start.3 = ((bf16[32,3,16,1024]{3,2,1,0:T(8,128)(2,1)}), bf16[32,3,16,1024]{3,2,1,0:T(8,128)(2,1)}, u32[]{:S(2)}, u32[]{:S(2)}) async-start(bf16[32,3,16,1024]{3,2,1,0:T(8,128)(2,1)} %bitcast.214), calls=%async_computation.3 | async-start | bytes 6291456 | tf_op jit(solution)/shard_map/all_to_all | solution.py:99
  207.4 4.2 copy-start.28
  207.4 4.5 copy-start.30
  212.8 4.5 copy-start.8
  213.0 8.8 %copy-start.14 = (f32[512,512]{0,1:T(8,128)}, f32[512,512]{0,1:T(8,128)S(1)}, u32[]{:S(2)}) copy-start(f32[512,512]{0,1:T(8,128)S(1)} %fusion.26) | copy-start | bytes 3145732
  278.4 6.3 copy-start.21
  284.8 5.1 copy-start.22
  284.8 10.1 %slice-start = ((s8[8388608]{0:T(1024)(128)(4,1)}), s8[4194304]{0:T(1024)(128)(4,1)S(1)}, s32[]{:S(2)}) async-start(s8[8388608]{0:T(1024)(128)(4,1)} %bitcast.206), calls=%async_computation.8 | async-start | bytes 8388608
  289.9 5.1 slice-start.1
  306.9 5.8 copy-start.4
  306.9 5.8 copy-start.6
  306.9 6.3 copy-start
  321.4 4.1 copy-start.16
  325.5 8.7 %copy-start.11 = (bf16[8,512,512]{1,2,0:T(8,128)(2,1)}, bf16[8,512,512]{1,2,0:T(8,128)(2,1)S(1)}, u32[]{:S(2)}) copy-start(bf16[8,512,512]{1,2,0:T(8,128)(2,1)S(1)} %fusion.2) | copy-start | bytes 12582916
  325.5 5.1 copy-start.3
  325.5 5.4 copy-start.18
  373.8 91.2 %all-to-all-start.4 = ((bf16[1,3,512,1024]{3,1,0,2:T(4,128)(2,1)}), bf16[1,3,512,1024]{3,1,0,2:T(4,128)(2,1)}, u32[]{:S(2)}, u32[]{:S(2)}) async-start(bf16[1,3,512,1024]{3,1,0,2:T(4,128)(2,1)} %pad_maximum_fusion), calls=%async_computation.4 | async-start | bytes 8388608 | tf_op jit(solution)/shard_map/all_to_all | solution.py:138
  465.0 95.9 %all-to-all-start.6 = ((bf16[1,3,512,1024]{3,1,0,2:T(4,128)(2,1)}), bf16[1,3,512,1024]{3,1,0,2:T(4,128)(2,1)}, u32[]{:S(2)}, u32[]{:S(2)}) async-start(bf16[1,3,512,1024]{3,1,0,2:T(4,128)(2,1)} %pad_maximum_fusion.1), calls=%async_computation.6 | async-start | bytes 8388608 | tf_op jit(solution)/shard_map/all_to_all | solution.py:139
  560.9 29.1 %all-to-all-start.5 = ((bf16[32,16,1024]{2,1,0:T(8,128)(2,1)}), bf16[32,16,1024]{2,1,0:T(8,128)(2,1)}, u32[]{:S(2)}, u32[]{:S(2)}) async-start(bf16[32,16,1024]{2,1,0:T(8,128)(2,1)} %copy.544), calls=%async_computation.5 | async-start | bytes 2097152 | tf_op jit(solution)/shard_map/all_to_all | solution.py:157
  573.6 4.5 copy-start.13
  573.6 4.7 copy-start.20
  590.0 125.0 %all-to-all-start.7 = ((bf16[32,16,1024]{2,1,0:T(8,128)(2,1)}), bf16[32,16,1024]{2,1,0:T(8,128)(2,1)S(1)}, u32[]{:S(2)}, u32[]{:S(2)}) async-start(bf16[32,16,1024]{2,1,0:T(8,128)(2,1)} %copy.562), calls=%async_computation.7 | async-start | bytes 2097152 | tf_op jit(solution)/shard_map/all_to_all | solution.py:160
  607.6 6.2 copy-start.25
  620.9 5.2 copy-start.10
  626.1 88.9 %copy-start.24 = (f32[1,512,1024]{2,1,0:T(8,128)S(1)}, f32[1,512,1024]{2,1,0:T(8,128)}, u32[]{:S(2)}) copy-start(f32[1,512,1024]{2,1,0:T(8,128)} %copy.563) | copy-start | bytes 6291460
  (12 other events, 35.6 us)
where the time goes:
time: 727 us; the launch traced here: 717 us
  waiting for transfers between devices  215 us (30%)
  local copies, waits for them, and re-layouts  138 us (19%)
  blocking collectives  134 us (18%)
  matrix products  94.3 us (13%)
  other arithmetic  66.9 us (9%)
  starting transfers between devices  65.5 us (9%)
    psum x1, blocking collectives, local(): lax.psum((query_gain_part, key_gain_part), ('dp', 'ctx'))  85 us
    all_to_all x1, waiting for transfers between devices, local(): lax.all_to_all(remote_value_all, 'ctx', split_axis=2, concat_axis=0, tile...  71.2 us
    all_to_all x1, waiting for transfers between devices, local(): lax.all_to_all(holder_keys[choice_table], 'ctx', split_axis=0, concat_axi...  54.6 us
    all_gather x1, blocking collectives, local(): choice_table = lax.all_gather(selected[0], 'ctx', axis=0, tiled=True)  48.7 us
    unnamed x88, local copies, waits for them, and re-layouts  44.6 us
    all_to_all x1, waiting for transfers between devices, local(): lax.all_to_all(remote_key_all, 'ctx', split_axis=2, concat_axis=0, tiled=...  42.1 us
    all_to_all x1, waiting for transfers between devices, local(): lax.all_to_all(holder_values[choice_table], 'ctx', split_axis=0, concat_a...  34.6 us
    unnamed x5, other arithmetic  21.1 us
  transfers between devices with their start and end apart: 8, of which 5 were waited for; matrix products, arithmetic and copies ran while one was open for 23% of the time, Pallas kernels for 0%

commit v1 on v0

--- a/solution.py
+++ b/solution.py
@@ -173,7 +173,9 @@
     query_grad, query_gain_part = query_pull(query_grads)
     _, key_pull = jax.vjp(head_norm, key_float, key_gain)
     key_grad, key_gain_part = key_pull(key_total)
-    query_gain_grad, key_gain_grad = lax.psum((query_gain_part, key_gain_part), ("dp", "ctx"))
+    query_gain_grad, key_gain_grad = lax.psum(
+        lax.psum((query_gain_part, key_gain_part), "ctx"), "dp"
+    )
     return (
         outputs[None],
         query_grad.astype(jnp.bfloat16)[None],

time: 727 us -> 740 us (1.018)
  blocking collectives: 134 us -> 146 us
    psum x1 -> x2, blocking collectives: 85 us -> 97.1 us  [the longest x1 61 us: local(): lax.psum((query_gain_part, key_gain_part), 'ctx')]
  transfers between devices with their start and end apart: 8 -> 8, of which waited for: 5 -> 5; matrix products, arithmetic and copies ran while one was open for 23% -> 22% of each run, Pallas kernels for 0% -> 0%
where the time goes in v1:
time: 740 us; the launch traced here: 729 us
  waiting for transfers between devices  215 us (29%)
  blocking collectives  146 us (20%)
  local copies, waits for them, and re-layouts  138 us (19%)
  matrix products  94.4 us (13%)
  other arithmetic  66.9 us (9%)
  starting transfers between devices  65.5 us (9%)
    all_to_all x1, waiting for transfers between devices, local(): lax.all_to_all(remote_value_all, 'ctx', split_axis=2, concat_axis=0, tile...  71.2 us
    psum x1, blocking collectives, local(): lax.psum((query_gain_part, key_gain_part), 'ctx')  61 us
    all_to_all x1, waiting for transfers between devices, local(): lax.all_to_all(holder_keys[choice_table], 'ctx', split_axis=0, concat_axi...  54.6 us
    all_gather x1, blocking collectives, local(): choice_table = lax.all_gather(selected[0], 'ctx', axis=0, tiled=True)  48.7 us
    unnamed x88, local copies, waits for them, and re-layouts  44.6 us
    all_to_all x1, waiting for transfers between devices, local(): lax.all_to_all(remote_key_all, 'ctx', split_axis=2, concat_axis=0, tiled=...  42.2 us
    psum x1, blocking collectives, local(): lax.psum(lax.psum((query_gain_part, key_gain_part), 'ctx'), 'dp')  36.2 us
    all_to_all x1, waiting for transfers between devices, local(): lax.all_to_all(holder_values[choice_table], 'ctx', split_axis=0, concat_a...  34.6 us
  transfers between devices with their start and end apart: 8, of which 5 were waited for; matrix products, arithmetic and copies ran while one was open for 22% of the time, Pallas kernels for 0%

profile of v1, /device:TPU:1, one launch (start us, length us, event | category | flops | bytes accessed | tf_op | source)
XLA Modules:
  0.0 729.0 jit_solution(7000824114189305384)
XLA Ops:
  13.3 9.1 %reduce.7 = bf16[512,1024]{1,0:T(8,128)(2,1)} reduce(bf16[512,1,1024]{2,1,0:T(2,128)(2,1)} %bitcast.237, bf16[]{:T(256)} %broadcast.153), dimensions={1}, to_apply=%bitcast.200.reduce_sub_computation | reduce | bytes 2097154
  25.0 12.2 %all-to-all-start = ((bf16[32,2,8192]{2,1,0:T(2,128)(2,1)}), bf16[32,2,8192]{2,1,0:T(2,128)(2,1)}, u32[]{:S(2)}, u32[]{:S(2)}) async-start(bf16[32,2,8192]{2,1,0:T(2,128)(2,1)} %reshape.270), calls=%async_computation | async-start | bytes 2097152 | tf_op jit(solution)/shard_map/all_to_all | solution.py:81
  40.1 8.0 %reduce.6 = bf16[512,1024]{1,0:T(8,128)(2,1)S(1)} reduce(bf16[512,1,1024]{2,1,0:T(2,128)(2,1)} %bitcast.238, bf16[]{:T(256)} %broadcast.153), dimensions={1}, to_apply=%bitcast.199.reduce_sub_computation | reduce | bytes 2097154
  49.8 12.0 %all-to-all-done = bf16[32,2,8192]{2,1,0:T(2,128)(2,1)} async-done(((bf16[32,2,8192]{2,1,0:T(2,128)(2,1)}), bf16[32,2,8192]{2,1,0:T(2,128)(2,1)}, u32[]{:S(2)}, u32[]{:S(2)}) %all-to-all-start) | async-done | bytes 1048608 | tf_op jit(solution)/shard_map/all_to_all | solution.py:81
  61.8 8.7 %all-to-all-start.2 = ((bf16[32,2,8192]{2,1,0:T(2,128)(2,1)}), bf16[32,2,8192]{2,1,0:T(2,128)(2,1)}, u32[]{:S(2)}, u32[]{:S(2)}) async-start(bf16[32,2,8192]{2,1,0:T(2,128)(2,1)} %reshape.268), calls=%async_computation.2 | async-start | bytes 2097152 | tf_op jit(solution)/shard_map/all_to_all | solution.py:88
  70.5 48.7 %all-gather = s32[32,1,3]{2,1,0:T(1,128)S(1)} all-gather(s32[1,1,3]{2,1,0:T(1,128)S(1)} %copy-done.32), channel_id=2, replica_groups=mesh['dp'=8,'ctx'=32] {'ctx'}, dimensions={0}, use_global_device_ids=true | all-gather | bytes 396 | tf_op jit(solution)/shard_map/all_gather | solution.py:74
  119.6 5.8 reshape.271
  129.9 5.3 all-to-all-start.1
  135.2 5.8 reshape.269
  145.5 54.6 %all-to-all-done.1 = bf16[32,3,16,1024]{3,2,1,0:T(8,128)(2,1)} async-done(((bf16[32,3,16,1024]{3,2,1,0:T(8,128)(2,1)}), bf16[32,3,16,1024]{3,2,1,0:T(8,128)(2,1)}, u32[]{:S(2)}, u32[]{:S(2)}) %all-to-all-start.1) | async-done | bytes 3145760 | tf_op jit(solution)/shard_map/all_to_all | solution.py:98
  200.1 5.4 all-to-all-start.3
  232.9 34.6 %all-to-all-done.3 = bf16[32,3,16,1024]{3,2,1,0:T(8,128)(2,1)} async-done(((bf16[32,3,16,1024]{3,2,1,0:T(8,128)(2,1)}), bf16[32,3,16,1024]{3,2,1,0:T(8,128)(2,1)}, u32[]{:S(2)}, u32[]{:S(2)}) %all-to-all-start.3) | async-done | bytes 3145760 | tf_op jit(solution)/shard_map/all_to_all | solution.py:99
  278.5 6.3 fusion.6
  284.9 5.1 fusion.5
  295.0 11.9 %divide_convert_fusion.3 = (bf16[8,512,512]{1,2,0:T(8,128)(2,1)S(1)}, bf16[8,512,512]{1,2,0:T(8,128)(2,1)S(1)}, bf16[8,512,512]{1,2,0:T(8,128)(2,1)S(1)}, bf16[8,512,512]{1,2,0:T(8,128)(2,1)S(1)}) fusion(f32[8,512,512]{1,2,0:T(8,128)S(1)} %bitcast.207, f32[8,512]{1,0:T(8,128)S(1)} %add_add_fusion.2, f32[512,512]{0,1:T(8,128)} %copy-done.14, ...), kind=kLoop, calls=%fused_computation.12 | loop fusion | flops 33554432 | bytes 51396620 | tf_op jit(solution)/shard_map/convert_element_type | solution.py:24
  336.7 6.0 copy.538
  347.4 6.0 copy.539
  358.0 6.1 copy.540
  364.2 9.7 %pad_maximum_fusion = bf16[1,3,512,1024]{3,1,0,2:T(4,128)(2,1)} fusion(bf16[1,1,512,1024]{3,1,0,2:T(2,128)(2,1)} %copy.540, bf16[1,1,512,1024]{3,1,0,2:T(2,128)(2,1)} %copy.539, bf16[1,1,512,1024]{3,1,0,2:T(2,128)(2,1)} %copy.538), kind=kLoop, calls=%fused_computation.21 | loop fusion | flops 9437184 | bytes 6291456 | tf_op jit(solution)/shard_map/stack | solution.py:126
  373.8 7.3 all-to-all-start.4
  385.7 6.1 copy.556
  396.4 6.0 copy.557
  407.1 6.1 copy.558
  413.2 9.7 %pad_maximum_fusion.1 = bf16[1,3,512,1024]{3,1,0,2:T(4,128)(2,1)} fusion(bf16[1,1,512,1024]{3,1,0,2:T(2,128)(2,1)} %copy.558, bf16[1,1,512,1024]{3,1,0,2:T(2,128)(2,1)} %copy.557, bf16[1,1,512,1024]{3,1,0,2:T(2,128)(2,1)} %copy.556), kind=kLoop, calls=%fused_computation.22 | loop fusion | flops 9437184 | bytes 6291456 | tf_op jit(solution)/shard_map/stack | solution.py:131
  422.9 42.2 %all-to-all-done.4 = bf16[1,3,512,1024]{3,1,0,2:T(4,128)(2,1)} async-done(((bf16[1,3,512,1024]{3,1,0,2:T(4,128)(2,1)}), bf16[1,3,512,1024]{3,1,0,2:T(4,128)(2,1)}, u32[]{:S(2)}, u32[]{:S(2)}) %all-to-all-start.4) | async-done | bytes 3145760 | tf_op jit(solution)/shard_map/all_to_all | solution.py:138
  465.0 9.8 %all-to-all-start.6 = ((bf16[1,3,512,1024]{3,1,0,2:T(4,128)(2,1)}), bf16[1,3,512,1024]{3,1,0,2:T(4,128)(2,1)}, u32[]{:S(2)}, u32[]{:S(2)}) async-start(bf16[1,3,512,1024]{3,1,0,2:T(4,128)(2,1)} %pad_maximum_fusion.1), calls=%async_computation.6 | async-start | bytes 8388608 | tf_op jit(solution)/shard_map/all_to_all | solution.py:139
  489.7 71.2 %all-to-all-done.6 = bf16[1,3,512,1024]{3,1,0,2:T(4,128)(2,1)} async-done(((bf16[1,3,512,1024]{3,1,0,2:T(4,128)(2,1)}), bf16[1,3,512,1024]{3,1,0,2:T(4,128)(2,1)}, u32[]{:S(2)}, u32[]{:S(2)}) %all-to-all-start.6) | async-done | bytes 3145760 | tf_op jit(solution)/shard_map/all_to_all | solution.py:139
  560.9 7.3 %all-to-all-start.5 = ((bf16[32,16,1024]{2,1,0:T(8,128)(2,1)}), bf16[32,16,1024]{2,1,0:T(8,128)(2,1)}, u32[]{:S(2)}, u32[]{:S(2)}) async-start(bf16[32,16,1024]{2,1,0:T(8,128)(2,1)} %copy.544), calls=%async_computation.5 | async-start | bytes 2097152 | tf_op jit(solution)/shard_map/all_to_all | solution.py:157
  590.1 9.6 %all-to-all-start.7 = ((bf16[32,16,1024]{2,1,0:T(8,128)(2,1)}), bf16[32,16,1024]{2,1,0:T(8,128)(2,1)S(1)}, u32[]{:S(2)}, u32[]{:S(2)}) async-start(bf16[32,16,1024]{2,1,0:T(8,128)(2,1)} %copy.562), calls=%async_computation.7 | async-start | bytes 2097152 | tf_op jit(solution)/shard_map/all_to_all | solution.py:160
  621.0 5.2 multiply_reduce_fusion.1
  630.1 61.0 %all-reduce = (f32[128]{0:T(128)S(1)}, f32[128]{0:T(128)S(1)}) all-reduce(f32[128]{0:T(128)S(1)} %get-tuple-element.56, f32[128]{0:T(128)S(1)} %get-tuple-element.54), channel_id=1, replica_groups=mesh['dp'=8,'ctx'=32] {'ctx'}, use_global_device_ids=true, to_apply=%region_9.0 | all-reduce | flops 256 | bytes 2048 | tf_op jit(solution)/shard_map/psum | solution.py:177
  691.1 36.2 %all-reduce.1 = (f32[128]{0:T(128)}, f32[128]{0:T(128)}) all-reduce(f32[128]{0:T(128)S(1)} %get-tuple-element.58, f32[128]{0:T(128)S(1)} %get-tuple-element.59), channel_id=1, replica_groups=mesh['dp'=8,'ctx'=32] {'dp'}, use_global_device_ids=true, to_apply=%region_10.0 | all-reduce | flops 256 | bytes 2048 | tf_op jit(solution)/shard_map/psum | solution.py:176
  (166 shorter events, 186.4 us)
Async XLA Ops:
  3.3 4.5 copy-start.31
  3.3 4.5 copy-start.26
  13.3 23.9 %copy-start.27 = (bf16[1,512,1024]{2,1,0:T(8,128)(2,1)S(1)}, bf16[1,512,1024]{2,1,0:T(8,128)(2,1)}, u32[]{:S(2)}) copy-start(bf16[1,512,1024]{2,1,0:T(8,128)(2,1)} %param.9) | copy-start | bytes 3145732
  25.0 36.8 %all-to-all-start = ((bf16[32,2,8192]{2,1,0:T(2,128)(2,1)}), bf16[32,2,8192]{2,1,0:T(2,128)(2,1)}, u32[]{:S(2)}, u32[]{:S(2)}) async-start(bf16[32,2,8192]{2,1,0:T(2,128)(2,1)} %reshape.270), calls=%async_computation | async-start | bytes 2097152 | tf_op jit(solution)/shard_map/all_to_all | solution.py:81
  40.1 30.3 %copy-start.32 = (s32[1,1,3]{2,1,0:T(1,128)S(1)}, s32[1,1,3]{2,1,0:T(1,128)}, u32[]{:S(2)}) copy-start(s32[1,1,3]{2,1,0:T(1,128)} %param.12) | copy-start | bytes 40
  61.8 68.1 %all-to-all-start.2 = ((bf16[32,2,8192]{2,1,0:T(2,128)(2,1)}), bf16[32,2,8192]{2,1,0:T(2,128)(2,1)}, u32[]{:S(2)}, u32[]{:S(2)}) async-start(bf16[32,2,8192]{2,1,0:T(2,128)(2,1)} %reshape.268), calls=%async_computation.2 | async-start | bytes 2097152 | tf_op jit(solution)/shard_map/all_to_all | solution.py:88
  129.9 70.3 %all-to-all-start.1 = ((bf16[32,3,16,1024]{3,2,1,0:T(8,128)(2,1)}), bf16[32,3,16,1024]{3,2,1,0:T(8,128)(2,1)}, u32[]{:S(2)}, u32[]{:S(2)}) async-start(bf16[32,3,16,1024]{3,2,1,0:T(8,128)(2,1)} %bitcast.215), calls=%async_computation.1 | async-start | bytes 6291456 | tf_op jit(solution)/shard_map/all_to_all | solution.py:98
  200.1 67.3 %all-to-all-start.3 = ((bf16[32,3,16,1024]{3,2,1,0:T(8,128)(2,1)}), bf16[32,3,16,1024]{3,2,1,0:T(8,128)(2,1)}, u32[]{:S(2)}, u32[]{:S(2)}) async-start(bf16[32,3,16,1024]{3,2,1,0:T(8,128)(2,1)} %bitcast.214), calls=%async_computation.3 | async-start | bytes 6291456 | tf_op jit(solution)/shard_map/all_to_all | solution.py:99
  207.4 4.2 copy-start.28
  207.4 4.5 copy-start.30
  212.9 4.5 copy-start.8
  213.0 8.8 %copy-start.14 = (f32[512,512]{0,1:T(8,128)}, f32[512,512]{0,1:T(8,128)S(1)}, u32[]{:S(2)}) copy-start(f32[512,512]{0,1:T(8,128)S(1)} %fusion.26) | copy-start | bytes 3145732
  278.5 6.4 copy-start.21
  284.9 5.1 copy-start.22
  284.9 10.1 %slice-start = ((s8[8388608]{0:T(1024)(128)(4,1)}), s8[4194304]{0:T(1024)(128)(4,1)S(1)}, s32[]{:S(2)}) async-start(s8[8388608]{0:T(1024)(128)(4,1)} %bitcast.206), calls=%async_computation.8 | async-start | bytes 8388608
  290.0 5.1 slice-start.1
  307.0 5.8 copy-start.4
  307.0 5.8 copy-start.6
  307.0 6.3 copy-start
  321.5 4.1 copy-start.16
  325.6 8.7 %copy-start.11 = (bf16[8,512,512]{1,2,0:T(8,128)(2,1)}, bf16[8,512,512]{1,2,0:T(8,128)(2,1)S(1)}, u32[]{:S(2)}) copy-start(bf16[8,512,512]{1,2,0:T(8,128)(2,1)S(1)} %fusion.2) | copy-start | bytes 12582916
  325.6 5.1 copy-start.3
  325.6 5.4 copy-start.18
  373.8 91.2 %all-to-all-start.4 = ((bf16[1,3,512,1024]{3,1,0,2:T(4,128)(2,1)}), bf16[1,3,512,1024]{3,1,0,2:T(4,128)(2,1)}, u32[]{:S(2)}, u32[]{:S(2)}) async-start(bf16[1,3,512,1024]{3,1,0,2:T(4,128)(2,1)} %pad_maximum_fusion), calls=%async_computation.4 | async-start | bytes 8388608 | tf_op jit(solution)/shard_map/all_to_all | solution.py:138
  465.0 95.9 %all-to-all-start.6 = ((bf16[1,3,512,1024]{3,1,0,2:T(4,128)(2,1)}), bf16[1,3,512,1024]{3,1,0,2:T(4,128)(2,1)}, u32[]{:S(2)}, u32[]{:S(2)}) async-start(bf16[1,3,512,1024]{3,1,0,2:T(4,128)(2,1)} %pad_maximum_fusion.1), calls=%async_computation.6 | async-start | bytes 8388608 | tf_op jit(solution)/shard_map/all_to_all | solution.py:139
  560.9 29.2 %all-to-all-start.5 = ((bf16[32,16,1024]{2,1,0:T(8,128)(2,1)}), bf16[32,16,1024]{2,1,0:T(8,128)(2,1)}, u32[]{:S(2)}, u32[]{:S(2)}) async-start(bf16[32,16,1024]{2,1,0:T(8,128)(2,1)} %copy.544), calls=%async_computation.5 | async-start | bytes 2097152 | tf_op jit(solution)/shard_map/all_to_all | solution.py:157
  573.6 4.5 copy-start.13
  573.6 4.7 copy-start.20
  590.1 137.1 %all-to-all-start.7 = ((bf16[32,16,1024]{2,1,0:T(8,128)(2,1)}), bf16[32,16,1024]{2,1,0:T(8,128)(2,1)S(1)}, u32[]{:S(2)}, u32[]{:S(2)}) async-start(bf16[32,16,1024]{2,1,0:T(8,128)(2,1)} %copy.562), calls=%async_computation.7 | async-start | bytes 2097152 | tf_op jit(solution)/shard_map/all_to_all | solution.py:160
  607.6 6.2 copy-start.25
  620.9 5.3 copy-start.10
  626.2 101.0 %copy-start.24 = (f32[1,512,1024]{2,1,0:T(8,128)S(1)}, f32[1,512,1024]{2,1,0:T(8,128)}, u32[]{:S(2)}) copy-start(f32[1,512,1024]{2,1,0:T(8,128)} %copy.563) | copy-start | bytes 6291460
  (12 other events, 35.6 us)
